TPU v7x, 512 devices: a whole 4x8x8 slice. The times are simulated.
512 devices in a mesh: section: 8 (over y), dp: 16 (over z, core), tensor: 4 (over x).
Axes of the slice: x: 4, y: 8, z: 8, core: 2. Of those that a mesh axis runs over, the one named last changes fastest.
Arguments:
- section_inputs: bfloat16 [8, 128, 2560], P('section', 'dp', 'tensor'), may hold values from -40 to 40
- entering: bfloat16 [1, 128, 2560], P(None, 'dp', 'tensor'), may hold values from -40 to 40
- grad_outputs: bfloat16 [8, 128, 2560], P('section', 'dp', 'tensor'), may hold values from -6 to 6
- arriving: bfloat16 [1, 128, 2560], P(None, 'dp', 'tensor'), may hold values from -6 to 6
- live_rows: int32 [1], replicated, may hold values from 64 to 128
- stashed_inputs: bfloat16 [8, 2, 128, 2560], P('section', None, 'dp', 'tensor'), may hold values from -40 to 40
- norm_gain: bfloat16 [8, 2560], P('section', 'tensor'), may hold values from 0.25 to 1.75
- up_weight: bfloat16 [8, 2560, 14336], P('section', 'tensor', 'dp'), may hold values from -0.125 to 0.125
- down_weight: bfloat16 [8, 14336, 2560], P('section', 'dp', 'tensor'), may hold values from -0.046875 to 0.046875
- held_blocks: int32 [8, 4, 16, 6], P('section', 'tensor'), may hold values from 0 to 69, as said below
- held_count: int32 [8, 4, 16], P('section', 'tensor'), may hold values from 1 to 6, as said below
- held_owner: int32 [8, 4, 16, 6], P('section', 'tensor'), may hold values from 0 to 15, as said below
- first_moment: float32 [8, 4, 16, 6, 128, 128], P('section', 'tensor', 'dp'), may hold values from -4 to 4
- second_moment: float32 [8, 4, 16, 6, 128, 128], P('section', 'tensor', 'dp'), may hold values from 0.01 to 1
Outputs:
- section_outputs: bfloat16 [8, 2, 128, 2560], P('section', None, 'dp', 'tensor')
- input_grads: bfloat16 [8, 2, 128, 2560], P('section', None, 'dp', 'tensor')
- first_next: float32 [8, 4, 16, 6, 128, 128], P('section', 'tensor', 'dp')
- second_next: float32 [8, 4, 16, 6, 128, 128], P('section', 'tensor', 'dp')
- update_direction: float32 [8, 4, 16, 6, 128, 128], P('section', 'tensor', 'dp')
Inputs may be any that keep to these rules, and one draw needn't show every extreme that they name: `held_blocks`: A number below 35 names a block of the device's up projection share, row-major over 5 x 7 blocks; the others, less 35, a block of its down projection share, row-major over 7 x 5 blocks. A device's first held_count entries are distinct; later entries are not used. `held_count`: some device of each section and tensor index lists 6 trainable blocks. `held_owner`: the owners of one device's trainable blocks are distinct and never the device itself. Each dp index owns at most 6 blocks of one section and tensor index, and some owns exactly 6.
All inputs are finite; a program needn't handle non-finite values.
Results may differ from a plain program's by a relative error of at most 0.015.
Values may be sent and summed in bfloat16 or wider, within the bound.
A program may use at most 64 MiB of HBM per device.

v0:
```python
import jax
import jax.numpy as jnp
from jax import lax
from jax.sharding import PartitionSpec as P

DW = 2560
BLK = 128
EPSILON = 1e-06


def from_behind(value, axis, steps):
    count = lax.axis_size(axis)
    leading, last = (max(0, -steps), min(count, count - steps))
    return lax.ppermute(value, axis, [(source, source + steps) for source in range(leading, last)])


def normed_product(rows_all, gain_row, up_matrix):
    widened = rows_all.astype(jnp.float32)
    squares = jnp.sum(widened * widened, axis=1)
    normed = (widened * gain_row.astype(jnp.float32)).astype(jnp.bfloat16)
    product = jnp.dot(normed, up_matrix, preferred_element_type=jnp.float32)
    return (normed, squares, product)


def scales_of(squares):
    return lax.rsqrt(squares / DW + EPSILON)


def activate(hidden):
    return (hidden * jax.nn.sigmoid(hidden)).astype(jnp.bfloat16)


def hidden_backward(hidden, act_grad, row_scales, product):
    sigmoid_part = jax.nn.sigmoid(hidden)
    hidden_grad = act_grad * sigmoid_part * (1.0 + hidden * (1.0 - sigmoid_part))
    scaled_grad = (hidden_grad * row_scales[:, None]).astype(jnp.bfloat16)
    scale_grad = jnp.sum(hidden_grad * product, axis=1)
    return (scaled_grad, scale_grad)


def times_transposed(left, right):
    return lax.dot_general(
        left, right, (((1,), (1,)), ((), ())), preferred_element_type=jnp.float32
    )


def body(
    section_inputs,
    entering,
    grad_outputs,
    arriving,
    live_rows,
    stashed_inputs,
    norm_gain,
    up_weight,
    down_weight,
    held_blocks,
    held_count,
    held_owner,
    first_moment,
    second_moment,
):
    section_count = lax.axis_size("section")
    section_index = lax.axis_index("section")
    dp_index = lax.axis_index("dp")
    dp_count = lax.axis_size("dp")
    turn_count = stashed_inputs.shape[1]
    local_rows = section_inputs.shape[1]
    row_total = local_rows * dp_count
    gain_row = norm_gain[0]
    up_matrix = up_weight[0]
    down_matrix = down_weight[0]
    channel_blocks = up_matrix.shape[0] // BLK
    hidden_blocks = up_matrix.shape[1] // BLK
    up_count = channel_blocks * hidden_blocks
    capacity = held_owner.shape[3]
    row_start = dp_index * local_rows
    held_list = lax.dynamic_index_in_dim(held_blocks[0, 0], dp_index, 0, keepdims=False)
    down_number = held_list - up_count
    is_up = held_list < up_count
    left_index = jnp.where(
        is_up, held_list // hidden_blocks, channel_blocks + down_number // channel_blocks
    )
    right_index = jnp.where(
        is_up, held_list % hidden_blocks, hidden_blocks + down_number % channel_blocks
    )
    forward_results = []
    rows_in = section_inputs[0]
    for turn in range(turn_count):
        if turn > 0:
            passed_rows = from_behind(forward_results[-1], "section", 1)
            rows_in = jnp.where(section_index == 0, entering[turn - 1], passed_rows)
        forward_rows_all = lax.all_gather(rows_in, "dp", axis=0, tiled=True)
        forward_normed, forward_squares, forward_product = normed_product(
            forward_rows_all, gain_row, up_matrix
        )
        forward_product, forward_squares = (
            lax.psum(forward_product.astype(jnp.bfloat16), "tensor").astype(jnp.float32),
            lax.psum(forward_squares.astype(jnp.bfloat16), "tensor").astype(jnp.float32),
        )
        forward_activated = activate(forward_product * scales_of(forward_squares)[:, None])
        mixed_rows = lax.psum_scatter(
            jnp.dot(forward_activated, down_matrix, preferred_element_type=jnp.float32).astype(
                jnp.bfloat16
            ),
            "dp",
            scatter_dimension=0,
            tiled=True,
        ).astype(jnp.float32)
        forward_results.append((rows_in.astype(jnp.float32) + mixed_rows).astype(jnp.bfloat16))
    row_ids = row_start + lax.iota(jnp.int32, local_rows)
    backward_results = []
    kept_grads = jnp.zeros((capacity, BLK, BLK), jnp.float32)
    grads_in = grad_outputs[0]
    for turn in range(turn_count):
        if turn > 0:
            passed_grads = from_behind(backward_results[-1], "section", -1)
            masked = jnp.where(
                (row_ids < live_rows[turn - 1])[:, None],
                arriving[turn - 1],
                jnp.zeros_like(arriving[turn - 1]),
            )
            grads_in = jnp.where(section_index == section_count - 1, masked, passed_grads)
        rows_local = stashed_inputs[0, turn]
        rows_all = lax.all_gather(rows_local, "dp", axis=0, tiled=True)
        grads_all = lax.all_gather(grads_in, "dp", axis=0, tiled=True)
        normed, squares, product = normed_product(rows_all, gain_row, up_matrix)
        act_grad = times_transposed(grads_all, down_matrix)
        product, squares, act_grad = lax.psum((product, squares, act_grad), "tensor")
        row_scales = scales_of(squares)
        hidden = product * row_scales[:, None]
        activated = activate(hidden)
        scaled_grad, scale_grad = hidden_backward(hidden, act_grad, row_scales, product)
        normed_part = times_transposed(scaled_grad, up_matrix)
        normed_grad = lax.psum_scatter(normed_part, "dp", scatter_dimension=0, tiled=True)
        scale_grad_rows = lax.psum_scatter(scale_grad, "dp", scatter_dimension=0, tiled=True)
        scale_rows = lax.dynamic_slice_in_dim(row_scales, row_start, local_rows, 0)
        widened = rows_local.astype(jnp.float32)
        input_grad = (
            grads_in.astype(jnp.float32)
            + normed_grad * gain_row.astype(jnp.float32)
            - (scale_grad_rows * scale_rows**3)[:, None] * widened / DW
        )
        left_table = jnp.concatenate(
            [
                normed.reshape(row_total, channel_blocks, BLK),
                activated.reshape(row_total, hidden_blocks, BLK),
            ],
            axis=1,
        )
        right_table = jnp.concatenate(
            [
                scaled_grad.reshape(row_total, hidden_blocks, BLK),
                grads_all.reshape(row_total, channel_blocks, BLK),
            ],
            axis=1,
        )
        left_pick = jnp.take(left_table, left_index, axis=1)
        right_pick = jnp.take(right_table, right_index, axis=1)
        block_grads = jnp.einsum(
            "rkb,rkc->kbc", left_pick, right_pick, preferred_element_type=jnp.float32
        )
        result, block_grads = (input_grad.astype(jnp.bfloat16), block_grads)
        backward_results.append(result)
        kept_grads = kept_grads + block_grads
    counts = held_count[0, 0]
    owners = held_owner[0, 0]
    slot_ids = lax.iota(jnp.int32, capacity)
    dp_ids = lax.iota(jnp.int32, dp_count)
    live_slots = slot_ids[None, :] < counts[:, None]
    chosen = (owners[:, None, :] == dp_ids[None, :, None]) & live_slots[:, None, :]
    is_sent = jnp.any(chosen, axis=2)
    slot_pick = jnp.sum(jnp.where(chosen, slot_ids[None, None, :], 0), axis=2)
    mine_sent = lax.dynamic_index_in_dim(is_sent, dp_index, 0, keepdims=False)
    mine_pick = lax.dynamic_index_in_dim(slot_pick, dp_index, 0, keepdims=False)
    outgoing = jnp.where(mine_sent[:, None, None], jnp.take(kept_grads, mine_pick, axis=0), 0.0)
    arrived = lax.all_to_all(outgoing, "dp", split_axis=0, concat_axis=0, tiled=True)
    from_source = lax.dynamic_index_in_dim(is_sent, dp_index, 1, keepdims=False)
    source_count = from_source.astype(jnp.int32)
    ranks = jnp.cumsum(source_count) - source_count
    matches = from_source[None, :] & (ranks[None, :] == slot_ids[:, None])
    is_filled = jnp.any(matches, axis=1)
    source_ids = jnp.sum(jnp.where(matches, dp_ids[None, :], 0), axis=1)
    owned_grads = jnp.where(is_filled[:, None, None], jnp.take(arrived, source_ids, axis=0), 0.0)
    filled = is_filled[:, None, None]
    first_new = 0.9 * first_moment[0, 0, 0] + 0.1 * owned_grads
    second_new = 0.999 * second_moment[0, 0, 0] + 0.001 * owned_grads * owned_grads
    direction = first_new / (jnp.sqrt(second_new) + 1e-08)
    first_out = jnp.where(filled, first_new, 0.0)
    second_out = jnp.where(filled, second_new, 0.0)
    direction_out = jnp.where(filled, direction, 0.0)
    section_rows = jnp.stack(forward_results)
    grad_rows = jnp.stack(backward_results)
    return (
        section_rows[None],
        grad_rows[None],
        first_out[None, None, None],
        second_out[None, None, None],
        direction_out[None, None, None],
    )


def solution(mesh):
    return jax.shard_map(
        body,
        mesh=mesh,
        in_specs=(
            P("section", "dp", "tensor"),
            P(None, "dp", "tensor"),
            P("section", "dp", "tensor"),
            P(None, "dp", "tensor"),
            P(),
            P("section", None, "dp", "tensor"),
            P("section", "tensor"),
            P("section", "tensor", "dp"),
            P("section", "dp", "tensor"),
            P("section", "tensor", None, None),
            P("section", "tensor", None),
            P("section", "tensor", None, None),
            P("section", "tensor", "dp", None, None, None),
            P("section", "tensor", "dp", None, None, None),
        ),
        out_specs=(
            P("section", None, "dp", "tensor"),
            P("section", None, "dp", "tensor"),
            P("section", "tensor", "dp", None, None, None),
            P("section", "tensor", "dp", None, None, None),
            P("section", "tensor", "dp", None, None, None),
        ),
        check_vma=False,
    )
```

profile of v0, /device:TPU:1, one launch (start us, length us, event | category | flops | bytes accessed | tf_op | source)
XLA Modules:
  0.0 778.5 jit_solution(2961250332882547614)
XLA Ops:
  8.8 24.9 %all-gather.2 = bf16[1,1,128,640]{3,2,1,0:T(8,128)(2,1)S(1)} all-gather(bf16[1,1,8,640]{3,2,1,0:T(8,128)(2,1)S(1)} %get-tuple-element.41), channel_id=4, replica_groups=mesh['section'=8,'dp'=16,'tensor'=4] {'dp'}, dimensions={2}, use_global_device_ids=true | all-gather | bytes 174080 | tf_op jit(solution)/shard_map/all_gather | solution.py:125
  33.9 15.2 %all-gather.1 = bf16[1,128,640]{2,1,0:T(8,128)(2,1)S(1)} all-gather(bf16[1,8,640]{2,1,0:T(8,128)(2,1)} %param.18), channel_id=3, replica_groups=mesh['section'=8,'dp'=16,'tensor'=4] {'dp'}, dimensions={1}, use_global_device_ids=true | all-gather | bytes 174080 | tf_op jit(solution)/shard_map/all_gather | solution.py:126
  49.0 16.2 %all-gather.3 = bf16[1,1,128,640]{3,2,1,0:T(8,128)(2,1)S(1)} all-gather(bf16[1,1,8,640]{3,2,1,0:T(8,128)(2,1)S(1)} %get-tuple-element.42), channel_id=5, replica_groups=mesh['section'=8,'dp'=16,'tensor'=4] {'dp'}, dimensions={2}, use_global_device_ids=true | all-gather | bytes 174080 | tf_op jit(solution)/shard_map/all_gather | solution.py:125
  68.1 14.9 %all-gather = bf16[1,128,640]{2,1,0:T(8,128)(2,1)S(1)} all-gather(bf16[1,8,640]{2,1,0:T(8,128)(2,1)S(1)} %copy-done.15), channel_id=2, replica_groups=mesh['section'=8,'dp'=16,'tensor'=4] {'dp'}, dimensions={1}, use_global_device_ids=true | all-gather | bytes 174080 | tf_op jit(solution)/shard_map/all_gather | solution.py:93
  83.2 8.9 %all-reduce.6 = (f32[128]{0:T(128)S(1)}, f32[128]{0:T(128)S(1)}) all-reduce(f32[128]{0:T(128)S(1)} %get-tuple-element.38, f32[128]{0:T(128)S(1)} %get-tuple-element.43), channel_id=1, replica_groups=mesh['section'=8,'dp'=16,'tensor'=4] {'tensor'}, use_global_device_ids=true, to_apply=%region_18.19 | all-reduce | flops 256 | bytes 2048 | tf_op jit(solution)/shard_map/psum | solution.py:129
  92.1 27.8 %all-reduce.32.cloned.1.call-done = (f32[128,896]{1,0:T(8,128)}, f32[128,896]{1,0:T(8,128)}) async-done(((f32[128,896]{1,0:T(8,128)}, f32[128,896]{1,0:T(8,128)}), (f32[128,896]{1,0:T(8,128)}, f32[128,896]{1,0:T(8,128)})) %all-reduce.32.cloned.1.call-update) | async-done | bytes 917520 | tf_op jit(solution)/shard_map/psum | solution.py:129
  119.9 1.6 multiply_reduce_fusion.1
  129.6 8.1 %psum.71 = bf16[128]{0:T(256)(128)(2,1)S(1)} all-reduce(bf16[128]{0:T(256)(128)(2,1)S(1)} %fusion.21), channel_id=1, replica_groups=mesh['section'=8,'dp'=16,'tensor'=4] {'tensor'}, use_global_device_ids=true, to_apply=%region_2.3 | all-reduce | flops 128 | bytes 512 | tf_op jit(solution)/shard_map/psum | solution.py:99
  140.8 28.0 %all-reduce.3 = f32[128]{0:T(128)S(1)} all-reduce(f32[128]{0:T(128)S(1)} %get-tuple-element.30), channel_id=9, replica_groups=mesh['section'=8,'dp'=16,'tensor'=4] {'dp'}, use_global_device_ids=true, to_apply=%region_14.15.clone | all-reduce | flops 128 | bytes 1024
  168.9 69.6 %all-reduce.26.cloned.1.call-done = f32[128,640]{1,0:T(8,128)} async-done(((f32[128,640]{1,0:T(8,128)}), f32[128,640]{1,0:T(8,128)}) %all-reduce.26.cloned.1.call-update) | async-done | bytes 327696
  239.4 1.4 collective-permute-start.1
  240.8 50.0 %all-reduce.18.cloned.1.call-done = bf16[128,896]{1,0:T(8,128)(2,1)} async-done(((bf16[128,896]{1,0:T(8,128)(2,1)}), bf16[128,896]{1,0:T(8,128)(2,1)}) %all-reduce.18.cloned.1.call-update) | async-done | bytes 229392 | tf_op jit(solution)/shard_map/psum | solution.py:98
  290.8 2.0 convolution_convert_fusion.3
  293.0 21.1 %all_gather.22 = bf16[128,640]{1,0:T(8,128)(2,1)S(1)} all-gather(bf16[8,640]{1,0:T(8,128)(2,1)S(1)} %fusion.63), channel_id=1, replica_groups=mesh['section'=8,'dp'=16,'tensor'=4] {'dp'}, dimensions={0}, use_global_device_ids=true | all-gather | bytes 174080 | tf_op jit(solution)/shard_map/all_gather | solution.py:126
  316.0 88.5 %all-reduce.22.cloned.1.call-done = bf16[128,640]{1,0:T(8,128)(2,1)} async-done(((bf16[128,640]{1,0:T(8,128)(2,1)}), bf16[128,640]{1,0:T(8,128)(2,1)}) %all-reduce.22.cloned.1.call-update) | async-done | bytes 163856
  405.3 3.1 collective-permute-start
  411.6 16.2 %all_gather.19 = bf16[128,640]{1,0:T(8,128)(2,1)S(1)} all-gather(bf16[8,640]{1,0:T(8,128)(2,1)S(1)} %bitcast_select_fusion.2), channel_id=1, replica_groups=mesh['section'=8,'dp'=16,'tensor'=4] {'dp'}, dimensions={0}, use_global_device_ids=true | all-gather | bytes 174080 | tf_op jit(solution)/shard_map/all_gather | solution.py:93
  434.0 26.0 %all-reduce.30.cloned.1.call-done = (f32[128,896]{1,0:T(8,128)}, f32[128,896]{1,0:T(8,128)}) async-done(((f32[128,896]{1,0:T(8,128)}, f32[128,896]{1,0:T(8,128)}), (f32[128,896]{1,0:T(8,128)}, f32[128,896]{1,0:T(8,128)})) %all-reduce.30.cloned.1.call-update) | async-done | bytes 917520 | tf_op jit(solution)/shard_map/psum | solution.py:129
  460.1 2.1 multiply_reduce_fusion
  464.3 1.4 gather_fusion.4
  467.7 1.4 gather_fusion.5
  469.1 1.4 convolution_add_fusion
  470.5 1.8 gather_fusion
  472.3 2.5 select_select_fusion
  474.7 9.7 %all-to-all-start = ((f32[16,128,128]{2,1,0:T(8,128)}), f32[16,128,128]{2,1,0:T(8,128)}, u32[]{:S(2)}, u32[]{:S(2)}) async-start(f32[16,128,128]{2,1,0:T(8,128)} %select_select_fusion), calls=%async_computation | async-start | bytes 2097152 | tf_op jit(solution)/shard_map/all_to_all | solution.py:177
  485.9 8.5 %psum.73 = bf16[128]{0:T(256)(128)(2,1)S(1)} all-reduce(bf16[128]{0:T(256)(128)(2,1)S(1)} %fusion.19), channel_id=1, replica_groups=mesh['section'=8,'dp'=16,'tensor'=4] {'tensor'}, use_global_device_ids=true, to_apply=%region_6.7 | all-reduce | flops 128 | bytes 512 | tf_op jit(solution)/shard_map/psum | solution.py:99
  494.4 43.6 %all-reduce.20.cloned.1.call-done = bf16[128,896]{1,0:T(8,128)(2,1)} async-done(((bf16[128,896]{1,0:T(8,128)(2,1)}), bf16[128,896]{1,0:T(8,128)(2,1)}) %all-reduce.20.cloned.1.call-update) | async-done | bytes 229392 | tf_op jit(solution)/shard_map/psum | solution.py:98
  538.1 2.0 convolution_convert_fusion.2
  540.2 111.8 %all-reduce.24.cloned.1.call-done = bf16[128,640]{1,0:T(8,128)(2,1)} async-done(((bf16[128,640]{1,0:T(8,128)(2,1)}), bf16[128,640]{1,0:T(8,128)(2,1)}) %all-reduce.24.cloned.1.call-update) | async-done | bytes 163856
  654.6 23.2 %all-reduce.5 = f32[128]{0:T(128)S(1)} all-reduce(f32[128]{0:T(128)S(1)} %copy-done.28), channel_id=11, replica_groups=mesh['section'=8,'dp'=16,'tensor'=4] {'dp'}, use_global_device_ids=true, to_apply=%region_21.22.clone | all-reduce | flops 128 | bytes 1024
  677.8 89.3 %all-reduce.28.cloned.1.call-done = f32[128,640]{1,0:T(8,128)} async-done(((f32[128,640]{1,0:T(8,128)}), f32[128,640]{1,0:T(8,128)}) %all-reduce.28.cloned.1.call-update) | async-done | bytes 327696
  768.5 1.8 gather_fusion.1
  (165 shorter events, 38.6 us)
Async XLA Ops:
  7.2 59.6 %copy-start = (bf16[1,640,896]{2,1,0:T(8,128)(2,1)S(1)}, bf16[1,640,896]{2,1,0:T(8,128)(2,1)}, u32[]{:S(2)}) copy-start(bf16[1,640,896]{2,1,0:T(8,128)(2,1)} %param.23) | copy-start | bytes 3440644
  7.2 58.2 %copy-start.1 = (bf16[1,896,640]{2,1,0:T(8,128)(2,1)S(1)}, bf16[1,896,640]{2,1,0:T(8,128)(2,1)}, u32[]{:S(2)}) copy-start(bf16[1,896,640]{2,1,0:T(8,128)(2,1)} %param.24) | copy-start | bytes 3440644
  7.2 112.7 %all-reduce.32.cloned.1.call-start = ((), (), s32[]{:S(2)}) async-start(), calls=%async_computation.8 | async-start | bytes 1835008 | tf_op jit(solution)/shard_map/psum | solution.py:129
  68.0 170.5 %all-reduce.26.cloned.1.call-start = ((), (), s32[]{:S(2)}) async-start(), calls=%async_computation.5 | async-start | bytes 655360
  122.7 168.1 %all-reduce.18.cloned.1.call-start = ((), (), s32[]{:S(2)}) async-start(), calls=%async_computation.1 | async-start | bytes 458752 | tf_op jit(solution)/shard_map/psum | solution.py:98
  124.0 114.6 %copy-start.8 = (bf16[1,2,8,640]{3,2,1,0:T(8,128)(2,1)S(1)}, bf16[1,2,8,640]{3,2,1,0:T(8,128)(2,1)}, u32[]{:S(2)}) copy-start(bf16[1,2,8,640]{3,2,1,0:T(8,128)(2,1)} %param.21) | copy-start | bytes 61444
  124.0 114.6 %copy-start.14 = (bf16[1,8,640]{2,1,0:T(8,128)(2,1)S(1)}, bf16[1,8,640]{2,1,0:T(8,128)(2,1)}, u32[]{:S(2)}) copy-start(bf16[1,8,640]{2,1,0:T(8,128)(2,1)} %param.18) | copy-start | bytes 30724
  124.0 280.6 %all-reduce.22.cloned.1.call-start = ((), (), s32[]{:S(2)}) async-start(), calls=%async_computation.3 | async-start | bytes 327680
  129.6 330.5 %copy-start.26 = (f32[128]{0:T(128)}, f32[128]{0:T(128)S(1)}, u32[]{:S(2)}) copy-start(f32[128]{0:T(128)S(1)} %add_rsqrt_fusion) | copy-start | bytes 1540
  140.8 291.9 %copy-start.21 = (pred[6]{0:T(512)(128)(4,1)}, pred[6]{0:T(512)(128)(4,1)S(1)}, u32[]{:S(2)}) copy-start(pred[6]{0:T(512)(128)(4,1)S(1)} %get-tuple-element.24) | copy-start | bytes 22
  140.8 291.9 %copy-start.23 = (pred[6]{0:T(512)(128)(4,1)}, pred[6]{0:T(512)(128)(4,1)S(1)}, u32[]{:S(2)}) copy-start(pred[6]{0:T(512)(128)(4,1)S(1)} %get-tuple-element.47) | copy-start | bytes 22
  140.8 289.7 %copy-start.20 = (s32[1024]{0:T(1024)}, s32[1024]{0:T(1024)S(1)}, u32[]{:S(2)}) copy-start(s32[1024]{0:T(1024)S(1)} %get-tuple-element.50) | copy-start | bytes 12292
  140.8 291.3 %copy-start.19 = (s32[1024]{0:T(1024)}, s32[1024]{0:T(1024)S(1)}, u32[]{:S(2)}) copy-start(s32[1024]{0:T(1024)S(1)} %get-tuple-element.49) | copy-start | bytes 12292
  239.4 53.5 %copy-start.17 = (bf16[1,8,640]{2,1,0:T(8,128)(2,1)S(1)}, bf16[1,8,640]{2,1,0:T(8,128)(2,1)}, u32[]{:S(2)}) copy-start(bf16[1,8,640]{2,1,0:T(8,128)(2,1)} %param.19) | copy-start | bytes 30724
  239.4 53.5 %collective-permute-start.1 = (bf16[8,640]{1,0:T(8,128)(2,1)S(1)}, bf16[8,640]{1,0:T(8,128)(2,1)S(1)}, u32[]{:S(2)}, u32[]{:S(2)}) collective-permute-start(bf16[8,640]{1,0:T(8,128)(2,1)S(1)} %fusion.58), channel_id=1, source_target_pairs={{64,0},{128,64},{192,128},{256,192},{320,256},{384,320},{448,384},... | collective-permute-start | bytes 30728 | tf_op jit(solution)/shard_map/ppermute | solution.py:14
  292.8 167.2 %all-reduce.30.cloned.1.call-start = ((), (), s32[]{:S(2)}) async-start(), calls=%async_computation.7 | async-start | bytes 1835008 | tf_op jit(solution)/shard_map/psum | solution.py:129
  316.0 95.6 %copy-start.18 = (bf16[1,8,640]{2,1,0:T(8,128)(2,1)S(1)}, bf16[1,8,640]{2,1,0:T(8,128)(2,1)}, u32[]{:S(2)}) copy-start(bf16[1,8,640]{2,1,0:T(8,128)(2,1)} %param.17) | copy-start | bytes 30724
  405.3 6.3 collective-permute-start
  474.7 293.8 %all-to-all-start = ((f32[16,128,128]{2,1,0:T(8,128)}), f32[16,128,128]{2,1,0:T(8,128)}, u32[]{:S(2)}, u32[]{:S(2)}) async-start(f32[16,128,128]{2,1,0:T(8,128)} %select_select_fusion), calls=%async_computation | async-start | bytes 2097152 | tf_op jit(solution)/shard_map/all_to_all | solution.py:177
  484.4 53.7 %all-reduce.20.cloned.1.call-start = ((), (), s32[]{:S(2)}) async-start(), calls=%async_computation.2 | async-start | bytes 458752 | tf_op jit(solution)/shard_map/psum | solution.py:98
  485.7 166.3 %all-reduce.24.cloned.1.call-start = ((), (), s32[]{:S(2)}) async-start(), calls=%async_computation.4 | async-start | bytes 327680
  494.4 157.6 %copy-start.7 = (bf16[8,640]{1,0:T(8,128)(2,1)S(1)}, bf16[8,640]{1,0:T(8,128)(2,1)}, u32[]{:S(2)}) copy-start(bf16[8,640]{1,0:T(8,128)(2,1)} %copy-done.6) | copy-start | bytes 30724
  540.1 113.8 %copy-start.13 = (bf16[8,640]{1,0:T(8,128)(2,1)S(1)}, bf16[8,640]{1,0:T(8,128)(2,1)}, u32[]{:S(2)}) copy-start(bf16[8,640]{1,0:T(8,128)(2,1)} %copy-done.12) | copy-start | bytes 30724
  540.1 114.5 %copy-start.28 = (f32[128]{0:T(128)S(1)}, f32[128]{0:T(128)}, u32[]{:S(2)}) copy-start(f32[128]{0:T(128)} %get-tuple-element.28) | copy-start | bytes 1540
  540.1 137.6 %copy-start.27 = (f32[128]{0:T(128)S(1)}, f32[128]{0:T(128)}, u32[]{:S(2)}) copy-start(f32[128]{0:T(128)} %copy-done.26) | copy-start | bytes 1540
  540.1 227.0 %copy-start.9 = (bf16[1,2,8,640]{3,2,1,0:T(8,128)(2,1)S(1)}, bf16[1,2,8,640]{3,2,1,0:T(8,128)(2,1)}, u32[]{:S(2)}) copy-start(bf16[1,2,8,640]{3,2,1,0:T(8,128)(2,1)} %param.21) | copy-start | bytes 61444
  540.1 227.8 %copy-start.11 = (bf16[8,640]{1,0:T(8,128)(2,1)S(1)}, bf16[8,640]{1,0:T(8,128)(2,1)}, u32[]{:S(2)}) copy-start(bf16[8,640]{1,0:T(8,128)(2,1)} %copy-done.10) | copy-start | bytes 30724
  540.2 226.9 %all-reduce.28.cloned.1.call-start = ((), (), s32[]{:S(2)}) async-start(), calls=%async_computation.6 | async-start | bytes 655360
  652.7 117.6 %copy-start.4 = (f32[1,1,1,6,128,128]{5,4,3,2,1,0:T(8,128)S(1)}, f32[1,1,1,6,128,128]{5,4,3,2,1,0:T(8,128)}, u32[]{:S(2)}) copy-start(f32[1,1,1,6,128,128]{5,4,3,2,1,0:T(8,128)} %param.28) | copy-start | bytes 1179652
  652.7 117.6 %copy-start.5 = (f32[1,1,1,6,128,128]{5,4,3,2,1,0:T(8,128)S(1)}, f32[1,1,1,6,128,128]{5,4,3,2,1,0:T(8,128)}, u32[]{:S(2)}) copy-start(f32[1,1,1,6,128,128]{5,4,3,2,1,0:T(8,128)} %param.29) | copy-start | bytes 1179652
  652.7 117.6 %copy-start.30 = (pred[6]{0:T(512)(128)(4,1)S(1)}, pred[6]{0:T(512)(128)(4,1)}, u32[]{:S(2)}) copy-start(pred[6]{0:T(512)(128)(4,1)} %fusion.65) | copy-start | bytes 22
  652.7 117.6 %copy-start.31 = (pred[6]{0:T(512)(128)(4,1)S(1)}, pred[6]{0:T(512)(128)(4,1)}, u32[]{:S(2)}) copy-start(pred[6]{0:T(512)(128)(4,1)} %compare_and_fusion.3) | copy-start | bytes 22
  (14 other events, 144.1 us)
Sparse Core Ops, SparseCore 0:
  68.2 51.6 all-reduce.31
  122.8 115.7 all-reduce.25
  241.6 49.1 all-reduce.17
  293.5 110.9 all-reduce.21
  406.9 53.0 all-reduce.29
  487.9 50.0 all-reduce.19
  541.0 110.9 all-reduce.23
  655.0 112.0 all-reduce.27
where the time goes:
time: 779 us; the launch traced here: 778 us
  waiting for transfers between devices  507 us (65%)
  blocking collectives  185 us (24%)
  other arithmetic  22 us (3%)
  local copies, waits for them, and re-layouts  18.4 us (2%)
  between operations  16 us (2%)
  matrix products  15.5 us (2%)
  starting transfers between devices  14.6 us (2%)
    unnamed x12, waiting for transfers between devices  359 us
    psum x2, waiting for transfers between devices, body(): lax.psum(forward_product.astype(jnp.bfloat16), 'tensor').astype(jnp.float32)  93.6 us
    psum x2, waiting for transfers between devices, body(): lax.psum((product, squares, act_grad), 'tensor')  53.8 us
    unnamed x2, blocking collectives  51.2 us
    all_gather x2, blocking collectives, body(): rows_all = lax.all_gather(rows_local, 'dp', axis=0, tiled=True)  41.1 us
    all_gather x2, blocking collectives, body(): grads_all = lax.all_gather(grads_in, 'dp', axis=0, tiled=True)  36.3 us
    all_gather x2, blocking collectives, body(): forward_rows_all = lax.all_gather(rows_in, 'dp', axis=0, tiled=True)  31.2 us
    psum x2, blocking collectives, body(): lax.psum(forward_squares.astype(jnp.bfloat16), 'tensor').astype(jnp.float32)  16.6 us
  transfers between devices with their start and end apart: 11, of which 8 were waited for; matrix products, arithmetic and copies ran while one was open for 4% of the time, Pallas kernels for 0%

commit v1 on v0

--- a/solution.py
+++ b/solution.py
@@ -6,6 +6,28 @@
 DW = 2560
 BLK = 128
 EPSILON = 1e-06
+
+
+def laid_out(pieces, dim):
+    pieces = jnp.moveaxis(pieces, 0, dim)
+    lengths = pieces.shape
+    return pieces.reshape(*lengths[:dim], lengths[dim] * lengths[dim + 1], *lengths[dim + 2 :])
+
+
+def ring_gather(value, axis, dim):
+    peers = lax.axis_size(axis)
+    pairs = [(i, (i + 1) % peers) for i in range(peers)]
+    back = [(b, a) for a, b in pairs]
+    lower, upper = ([], [])
+    for step in range(peers - 1):
+        if step % 2 == 0:
+            lower.append(lax.ppermute(lower[-1] if lower else value, axis, pairs))
+        else:
+            upper.append(lax.ppermute(upper[-1] if upper else value, axis, back))
+    tiles = jnp.stack([*lower[::-1], value, *upper])
+    shift = lax.axis_index(axis) - len(lower)
+    tiles = tiles[(jnp.arange(peers) - shift) % peers]
+    return laid_out(tiles, dim)
 
 
 def from_behind(value, axis, steps):
@@ -90,7 +112,7 @@
         if turn > 0:
             passed_rows = from_behind(forward_results[-1], "section", 1)
             rows_in = jnp.where(section_index == 0, entering[turn - 1], passed_rows)
-        forward_rows_all = lax.all_gather(rows_in, "dp", axis=0, tiled=True)
+        forward_rows_all = ring_gather(rows_in, "dp", 0)
         forward_normed, forward_squares, forward_product = normed_product(
             forward_rows_all, gain_row, up_matrix
         )

time: 779 us -> 828 us (1.063)
  starting transfers between devices: 14.6 us -> 60.5 us
  blocking collectives: 185 us -> 142 us
  waiting for transfers between devices: 507 us -> 548 us
    ppermute x0 -> x30, starting transfers between devices: none -> 46.1 us  [the longest x14 26.7 us: ring_gather(): upper.append(lax.ppermute(upper[-1] if upper else value, axis, back))]
    all_gather x2 -> x0, blocking collectives: 31.2 us -> none  [body(): forward_rows_all = lax.all_gather(rows_in, 'dp', axis=0, tiled=True)]
    unnamed x12, waiting for transfers between devices: 359 us -> 386 us
    ppermute x0 -> x30, waiting for transfers between devices: none -> 9.26 us  [the longest x14 6.06 us: ring_gather(): upper.append(lax.ppermute(upper[-1] if upper else value, axis, back))]
    all_gather x2, blocking collectives: 41.1 us -> 32.3 us  [body(): rows_all = lax.all_gather(rows_local, 'dp', axis=0, tiled=True)]
  transfers between devices with their start and end apart: 11 -> 41, of which waited for: 8 -> 21; matrix products, arithmetic and copies ran while one was open for 4% -> 5% of each run, Pallas kernels for 0% -> 0%
where the time goes in v1:
time: 828 us; the launch traced here: 827 us
  waiting for transfers between devices  548 us (66%)
  blocking collectives  142 us (17%)
  starting transfers between devices  60.5 us (7%)
  other arithmetic  22.4 us (3%)
  local copies, waits for them, and re-layouts  21.1 us (3%)
  matrix products  17.3 us (2%)
  between operations  16 us (2%)
    unnamed x12, waiting for transfers between devices  386 us
    psum x2, waiting for transfers between devices, body(): lax.psum(forward_product.astype(jnp.bfloat16), 'tensor').astype(jnp.float32)  86.4 us
    psum x2, waiting for transfers between devices, body(): lax.psum((product, squares, act_grad), 'tensor')  61.6 us
    unnamed x2, blocking collectives  49.5 us
    all_gather x2, blocking collectives, body(): grads_all = lax.all_gather(grads_in, 'dp', axis=0, tiled=True)  36.1 us
    all_gather x2, blocking collectives, body(): rows_all = lax.all_gather(rows_local, 'dp', axis=0, tiled=True)  32.3 us
    ppermute x14, starting transfers between devices, ring_gather(): upper.append(lax.ppermute(upper[-1] if upper else value, axis, back))  26.7 us
    ppermute x16, starting transfers between devices, ring_gather(): lower.append(lax.ppermute(lower[-1] if lower else value, axis, pairs))  19.4 us
  transfers between devices with their start and end apart: 41, of which 21 were waited for; matrix products, arithmetic and copies ran while one was open for 5% of the time, Pallas kernels for 0%

profile of v1, /device:TPU:1, one launch (start us, length us, event | category | flops | bytes accessed | tf_op | source)
XLA Modules:
  0.0 827.4 jit_solution(1627840274883081096)
XLA Ops:
  7.2 3.5 collective-permute-start
  10.7 3.4 collective-permute-start.8
  14.2 20.0 %all-gather = bf16[1,128,640]{2,1,0:T(8,128)(2,1)S(1)} all-gather(bf16[1,8,640]{2,1,0:T(8,128)(2,1)} %param.18), channel_id=2, replica_groups=mesh['section'=8,'dp'=16,'tensor'=4] {'dp'}, dimensions={1}, use_global_device_ids=true | all-gather | bytes 174080 | tf_op jit(solution)/shard_map/all_gather | solution.py:148
  34.2 2.5 fusion.2
  42.9 17.0 %all-gather.1 = bf16[1,1,128,640]{3,2,1,0:T(8,128)(2,1)S(1)} all-gather(bf16[1,1,8,640]{3,2,1,0:T(8,128)(2,1)S(1)} %get-tuple-element.41), channel_id=3, replica_groups=mesh['section'=8,'dp'=16,'tensor'=4] {'dp'}, dimensions={2}, use_global_device_ids=true | all-gather | bytes 174080 | tf_op jit(solution)/shard_map/all_gather | solution.py:147
  61.8 15.3 %all-gather.2 = bf16[1,1,128,640]{3,2,1,0:T(8,128)(2,1)S(1)} all-gather(bf16[1,1,8,640]{3,2,1,0:T(8,128)(2,1)S(1)} %get-tuple-element.42), channel_id=4, replica_groups=mesh['section'=8,'dp'=16,'tensor'=4] {'dp'}, dimensions={2}, use_global_device_ids=true | all-gather | bytes 174080 | tf_op jit(solution)/shard_map/all_gather | solution.py:147
  92.1 8.5 %psum.71 = bf16[128]{0:T(256)(128)(2,1)S(1)} all-reduce(bf16[128]{0:T(256)(128)(2,1)S(1)} %convert_element_type.172), channel_id=1, replica_groups=mesh['section'=8,'dp'=16,'tensor'=4] {'tensor'}, use_global_device_ids=true, to_apply=%region_2.3 | all-reduce | flops 128 | bytes 512 | tf_op jit(solution)/shard_map/psum | solution.py:121
  100.6 42.8 %all-reduce.18.cloned.1.call-done = bf16[128,896]{1,0:T(8,128)(2,1)} async-done(((bf16[128,896]{1,0:T(8,128)(2,1)}), bf16[128,896]{1,0:T(8,128)(2,1)}) %all-reduce.18.cloned.1.call-update) | async-done | bytes 229392 | tf_op jit(solution)/shard_map/psum | solution.py:120
  149.6 7.5 all-reduce.6
  161.4 96.0 %all-reduce.22.cloned.1.call-done = bf16[128,640]{1,0:T(8,128)(2,1)} async-done(((bf16[128,640]{1,0:T(8,128)(2,1)}), bf16[128,640]{1,0:T(8,128)(2,1)}) %all-reduce.22.cloned.1.call-update) | async-done | bytes 163856
  258.1 3.1 collective-permute-start.15
  264.8 2.3 collective-permute-start.17
  268.1 2.1 collective-permute-start.18
  273.9 2.8 collective-permute-start.26
  277.5 3.5 collective-permute-start.27
  281.8 3.8 collective-permute-start.28
  286.9 3.3 collective-permute-start.29
  292.8 3.0 collective-permute-start.30
  296.0 16.9 %all-reduce.32.cloned.1.call-done = (f32[128,896]{1,0:T(8,128)}, f32[128,896]{1,0:T(8,128)}) async-done(((f32[128,896]{1,0:T(8,128)}, f32[128,896]{1,0:T(8,128)}), (f32[128,896]{1,0:T(8,128)}, f32[128,896]{1,0:T(8,128)})) %all-reduce.32.cloned.1.call-update) | async-done | bytes 917520 | tf_op jit(solution)/shard_map/psum | solution.py:151
  315.7 26.3 %all-reduce.3 = f32[128]{0:T(128)S(1)} all-reduce(f32[128]{0:T(128)S(1)} %get-tuple-element.30), channel_id=8, replica_groups=mesh['section'=8,'dp'=16,'tensor'=4] {'dp'}, use_global_device_ids=true, to_apply=%region_14.15.clone | all-reduce | flops 128 | bytes 1024
  342.1 89.3 %all-reduce.26.cloned.1.call-done = f32[128,640]{1,0:T(8,128)} async-done(((f32[128,640]{1,0:T(8,128)}), f32[128,640]{1,0:T(8,128)}) %all-reduce.26.cloned.1.call-update) | async-done | bytes 327696
  433.6 3.1 collective-permute-done.31
  436.8 16.1 %all_gather.14 = bf16[128,640]{1,0:T(8,128)(2,1)S(1)} all-gather(bf16[8,640]{1,0:T(8,128)(2,1)S(1)} %fusion.63), channel_id=1, replica_groups=mesh['section'=8,'dp'=16,'tensor'=4] {'dp'}, dimensions={0}, use_global_device_ids=true | all-gather | bytes 174080 | tf_op jit(solution)/shard_map/all_gather | solution.py:148
  463.0 44.8 %all-reduce.30.cloned.1.call-done = (f32[128,896]{1,0:T(8,128)}, f32[128,896]{1,0:T(8,128)}) async-done(((f32[128,896]{1,0:T(8,128)}, f32[128,896]{1,0:T(8,128)}), (f32[128,896]{1,0:T(8,128)}, f32[128,896]{1,0:T(8,128)})) %all-reduce.30.cloned.1.call-update) | async-done | bytes 917520 | tf_op jit(solution)/shard_map/psum | solution.py:151
  507.7 2.1 multiply_reduce_fusion
  521.2 2.5 select_select_fusion
  523.7 9.7 %all-to-all-start = ((f32[16,128,128]{2,1,0:T(8,128)}), f32[16,128,128]{2,1,0:T(8,128)}, u32[]{:S(2)}, u32[]{:S(2)}) async-start(f32[16,128,128]{2,1,0:T(8,128)} %select_select_fusion), calls=%async_computation | async-start | bytes 2097152 | tf_op jit(solution)/shard_map/all_to_all | solution.py:199
  534.8 8.6 %psum.73 = bf16[128]{0:T(256)(128)(2,1)S(1)} all-reduce(bf16[128]{0:T(256)(128)(2,1)S(1)} %convert_element_type.185), channel_id=1, replica_groups=mesh['section'=8,'dp'=16,'tensor'=4] {'tensor'}, use_global_device_ids=true, to_apply=%region_6.7 | all-reduce | flops 128 | bytes 512 | tf_op jit(solution)/shard_map/psum | solution.py:121
  543.4 43.7 %all-reduce.20.cloned.1.call-done = bf16[128,896]{1,0:T(8,128)(2,1)} async-done(((bf16[128,896]{1,0:T(8,128)(2,1)}), bf16[128,896]{1,0:T(8,128)(2,1)}) %all-reduce.20.cloned.1.call-update) | async-done | bytes 229392 | tf_op jit(solution)/shard_map/psum | solution.py:120
  589.2 111.8 %all-reduce.24.cloned.1.call-done = bf16[128,640]{1,0:T(8,128)(2,1)} async-done(((bf16[128,640]{1,0:T(8,128)(2,1)}), bf16[128,640]{1,0:T(8,128)(2,1)}) %all-reduce.24.cloned.1.call-update) | async-done | bytes 163856
  703.5 23.2 %all-reduce.5 = f32[128]{0:T(128)S(1)} all-reduce(f32[128]{0:T(128)S(1)} %copy-done.17), channel_id=10, replica_groups=mesh['section'=8,'dp'=16,'tensor'=4] {'dp'}, use_global_device_ids=true, to_apply=%region_21.22.clone | all-reduce | flops 128 | bytes 1024
  726.8 89.3 %all-reduce.28.cloned.1.call-done = f32[128,640]{1,0:T(8,128)} async-done(((f32[128,640]{1,0:T(8,128)}), f32[128,640]{1,0:T(8,128)}) %all-reduce.28.cloned.1.call-update) | async-done | bytes 327696
  (237 shorter events, 83.8 us)
Async XLA Ops:
  7.2 136.1 %all-reduce.18.cloned.1.call-start = ((), (), s32[]{:S(2)}) async-start(), calls=%async_computation.1 | async-start | bytes 458752 | tf_op jit(solution)/shard_map/psum | solution.py:120
  7.2 29.4 %collective-permute-start = (bf16[8,640]{1,0:T(8,128)(2,1)}, bf16[8,640]{1,0:T(8,128)(2,1)S(1)}, u32[]{:S(2)}, u32[]{:S(2)}) collective-permute-start(bf16[8,640]{1,0:T(8,128)(2,1)} %bitcast.200), channel_id=1, source_target_pairs={{0,4},{4,8},{8,12},{12,16},{16,20},{20,24},{24,28},{28,32},{32,36}... | collective-permute-start | bytes 30728 | tf_op jit(solution)/shard_map/ppermute | solution.py:24
  10.7 29.0 %collective-permute-start.8 = (bf16[8,640]{1,0:T(8,128)(2,1)}, bf16[8,640]{1,0:T(8,128)(2,1)S(1)}, u32[]{:S(2)}, u32[]{:S(2)}) collective-permute-start(bf16[8,640]{1,0:T(8,128)(2,1)} %bitcast.201), channel_id=1, source_target_pairs={{4,0},{8,4},{12,8},{16,12},{20,16},{24,20},{28,24},{32,28},{36,32}... | collective-permute-start | bytes 30728 | tf_op jit(solution)/shard_map/ppermute | solution.py:26
  37.8 4.0 collective-permute-start.2
  39.8 20.1 %collective-permute-start.9 = (bf16[8,640]{1,0:T(8,128)(2,1)S(1)}, bf16[8,640]{1,0:T(8,128)(2,1)S(1)}, u32[]{:S(2)}, u32[]{:S(2)}) collective-permute-start(bf16[8,640]{1,0:T(8,128)(2,1)S(1)} %collective-permute-done.8), channel_id=1, source_target_pairs={{4,0},{8,4},{12,8},{16,12},{20,16},{24,20},{28,24},{32,28},{36,32}... | collective-permute-start | bytes 30728 | tf_op jit(solution)/shard_map/ppermute | solution.py:26
  41.8 18.2 %collective-permute-start.3 = (bf16[8,640]{1,0:T(8,128)(2,1)S(1)}, bf16[8,640]{1,0:T(8,128)(2,1)S(1)}, u32[]{:S(2)}, u32[]{:S(2)}) collective-permute-start(bf16[8,640]{1,0:T(8,128)(2,1)S(1)} %collective-permute-done.2), channel_id=1, source_target_pairs={{0,4},{4,8},{8,12},{12,16},{16,20},{20,24},{24,28},{28,32},{32,36}... | collective-permute-start | bytes 30728 | tf_op jit(solution)/shard_map/ppermute | solution.py:24
  59.9 17.5 %collective-permute-start.10 = (bf16[8,640]{1,0:T(8,128)(2,1)S(1)}, bf16[8,640]{1,0:T(8,128)(2,1)S(1)}, u32[]{:S(2)}, u32[]{:S(2)}) collective-permute-start(bf16[8,640]{1,0:T(8,128)(2,1)S(1)} %collective-permute-done.9), channel_id=1, source_target_pairs={{4,0},{8,4},{12,8},{16,12},{20,16},{24,20},{28,24},{32,28},{36,32}... | collective-permute-start | bytes 30728 | tf_op jit(solution)/shard_map/ppermute | solution.py:26
  60.0 17.5 %collective-permute-start.4 = (bf16[8,640]{1,0:T(8,128)(2,1)S(1)}, bf16[8,640]{1,0:T(8,128)(2,1)S(1)}, u32[]{:S(2)}, u32[]{:S(2)}) collective-permute-start(bf16[8,640]{1,0:T(8,128)(2,1)S(1)} %collective-permute-done.3), channel_id=1, source_target_pairs={{0,4},{4,8},{8,12},{12,16},{16,20},{20,24},{24,28},{28,32},{32,36}... | collective-permute-start | bytes 30728 | tf_op jit(solution)/shard_map/ppermute | solution.py:24
  80.5 4.3 collective-permute-start.6
  84.8 4.3 collective-permute-start.7
  91.8 165.6 %all-reduce.22.cloned.1.call-start = ((), (), s32[]{:S(2)}) async-start(), calls=%async_computation.3 | async-start | bytes 327680
  145.4 167.5 %all-reduce.32.cloned.1.call-start = ((), (), s32[]{:S(2)}) async-start(), calls=%async_computation.8 | async-start | bytes 1835008 | tf_op jit(solution)/shard_map/psum | solution.py:151
  146.7 284.8 %all-reduce.26.cloned.1.call-start = ((), (), s32[]{:S(2)}) async-start(), calls=%async_computation.5 | async-start | bytes 655360
  258.1 3.9 collective-permute-start.15
  267.1 3.7 collective-permute-start.24
  268.1 4.3 collective-permute-start.18
  272.4 4.3 collective-permute-start.19
  273.9 3.6 collective-permute-start.26
  276.7 4.3 collective-permute-start.20
  277.5 4.3 collective-permute-start.27
  281.0 4.7 collective-permute-start.21
  281.8 5.1 collective-permute-start.28
  285.7 4.5 collective-permute-start.22
  286.9 5.9 collective-permute-start.29
  290.2 5.7 collective-permute-start.23
  292.8 161.3 %collective-permute-start.30 = (bf16[8,640]{1,0:T(8,128)(2,1)S(1)}, bf16[8,640]{1,0:T(8,128)(2,1)S(1)}, u32[]{:S(2)}, u32[]{:S(2)}) collective-permute-start(bf16[8,640]{1,0:T(8,128)(2,1)S(1)} %collective-permute-done.29), channel_id=1, source_target_pairs={{4,0},{8,4},{12,8},{16,12},{20,16},{24,20},{28,24},{32,28},{36,32}... | collective-permute-start | bytes 30728 | tf_op jit(solution)/shard_map/ppermute | solution.py:26
  315.7 192.0 %all-reduce.30.cloned.1.call-start = ((), (), s32[]{:S(2)}) async-start(), calls=%async_computation.7 | async-start | bytes 1835008 | tf_op jit(solution)/shard_map/psum | solution.py:151
  432.3 4.4 collective-permute-start.31
  523.7 293.8 %all-to-all-start = ((f32[16,128,128]{2,1,0:T(8,128)}), f32[16,128,128]{2,1,0:T(8,128)}, u32[]{:S(2)}, u32[]{:S(2)}) async-start(f32[16,128,128]{2,1,0:T(8,128)} %select_select_fusion), calls=%async_computation | async-start | bytes 2097152 | tf_op jit(solution)/shard_map/all_to_all | solution.py:199
  533.4 53.7 %all-reduce.20.cloned.1.call-start = ((), (), s32[]{:S(2)}) async-start(), calls=%async_computation.2 | async-start | bytes 458752 | tf_op jit(solution)/shard_map/psum | solution.py:120
  534.6 166.4 %all-reduce.24.cloned.1.call-start = ((), (), s32[]{:S(2)}) async-start(), calls=%async_computation.4 | async-start | bytes 327680
  589.1 227.0 %all-reduce.28.cloned.1.call-start = ((), (), s32[]{:S(2)}) async-start(), calls=%async_computation.6 | async-start | bytes 655360
  (33 other events, 1423.6 us)
Sparse Core Ops, SparseCore 0:
  91.9 51.3 all-reduce.17
  146.3 110.9 all-reduce.21
  259.8 53.0 all-reduce.31
  315.8 115.6 all-reduce.25
  454.2 53.4 all-reduce.29
  536.9 50.0 all-reduce.19
  590.0 110.9 all-reduce.23
  704.0 112.0 all-reduce.27
